TPU v7x, 32 devices: a whole 2x2x4 slice. The times are simulated.
32 devices in a mesh: fsdp: 32 (over z, y, x, core).
Axes of the slice: x: 2, y: 2, z: 4, core: 2. Of those that a mesh axis runs over, the one named last changes fastest.
Arguments:
- layer_input: bfloat16 [96, 288, 768], P('fsdp'), may hold values from -6 to 6
- segments: int32 [96, 288], P('fsdp'), may hold values from 0 to 8, as said below
- cotangent: bfloat16 [96, 288, 768], P('fsdp'), may hold values from -6 to 6
- pre_gain: float32 [768], P('fsdp'), may hold values from 0.5 to 1.5
- pre_shift: float32 [768], P('fsdp'), may hold values from -2 to 2
- w_qkv: float32 [768, 2304], P('fsdp'), may hold values from -0.21875 to 0.21875
- b_query: float32 [768], P('fsdp'), may hold values from -3 to 3
- b_value: float32 [768], P('fsdp'), may hold values from -3 to 3
- w_out: float32 [768, 768], P('fsdp'), may hold values from -1.25 to 1.25
- b_out: float32 [768], P('fsdp'), may hold values from -3 to 3
- mid_gain: float32 [768], P('fsdp'), may hold values from 0.5 to 1.5
- mid_shift: float32 [768], P('fsdp'), may hold values from -2 to 2
- w_up: float32 [768, 3072], P('fsdp'), may hold values from -0.21875 to 0.21875
- b_up: float32 [3072], P('fsdp'), may hold values from -3 to 3
- w_down: float32 [3072, 768], P('fsdp'), may hold values from -0.109375 to 0.109375
- b_down: float32 [768], P('fsdp'), may hold values from -3 to 3
Outputs:
- layer_output: bfloat16 [96, 288, 768], P('fsdp')
- grad_input: bfloat16 [96, 288, 768], P('fsdp')
- grad_pre_gain: float32 [768], P('fsdp')
- grad_pre_shift: float32 [768], P('fsdp')
- grad_w_qkv: float32 [768, 2304], P('fsdp')
- grad_b_query: float32 [768], P('fsdp')
- grad_b_value: float32 [768], P('fsdp')
- grad_w_out: float32 [768, 768], P('fsdp')
- grad_b_out: float32 [768], P('fsdp')
- grad_mid_gain: float32 [768], P('fsdp')
- grad_mid_shift: float32 [768], P('fsdp')
- grad_w_up: float32 [768, 3072], P('fsdp')
- grad_b_up: float32 [3072], P('fsdp')
- grad_w_down: float32 [3072, 768], P('fsdp')
- grad_b_down: float32 [768], P('fsdp')
Inputs may be any that keep to these rules, and one draw needn't show every extreme that they name: `segments`: each row holds 8 or 7 images of 36 slots each, in slot order and numbered from 1; the remaining slots of a row are padding (0).
All inputs are finite; a program needn't handle non-finite values.
Results may differ from a plain program's by a relative error of at most 0.012.
The roundings to bfloat16 on the way count: a program that leaves them out, or rounds other values in their place, can miss the bound.
Values may be sent and summed in bfloat16 or wider, within the bound.
No kernel may reach another device: no remote copies, remote signals or barrier semaphores. Data moves between devices by JAX's collectives and lax.ppermute only.
A program may use at most 192 MiB of HBM per device.

v0:
```python
import jax
import jax.numpy as jnp
from jax import lax
from jax.sharding import PartitionSpec as P

HEAD_DIM = 64
PATCHES = 36
EPSILON = 1e-06


def norm_layer(value, gain, shift):
    average = jnp.mean(value, axis=-1, keepdims=True)
    centred = value - average
    spread = jnp.mean(centred * centred, axis=-1, keepdims=True)
    return centred * lax.rsqrt(spread + EPSILON) * gain + shift


def gelu_exact(value):
    return jax.nn.gelu(value, approximate=False)


def column_sums(value):
    return jnp.sum(value.astype(jnp.float32), axis=0)


def shards(
    layer_input,
    segments,
    cotangent,
    pre_gain,
    pre_shift,
    w_qkv,
    b_query,
    b_value,
    w_out,
    b_out,
    mid_gain,
    mid_shift,
    w_up,
    b_up,
    w_down,
    b_down,
):
    row_count, slot_count, model_width = layer_input.shape
    head_count = model_width // HEAD_DIM
    tokens = row_count * slot_count
    images = slot_count // PATCHES
    scaling = HEAD_DIM ** (-0.5)
    tiled = (row_count, images, PATCHES, head_count, HEAD_DIM)
    attn_full = (
        lax.all_gather(pre_gain.astype(jnp.bfloat16), "fsdp", axis=0, tiled=True),
        lax.all_gather(pre_shift.astype(jnp.bfloat16), "fsdp", axis=0, tiled=True),
        lax.all_gather(w_qkv.astype(jnp.bfloat16), "fsdp", axis=0, tiled=True),
        lax.all_gather(b_query.astype(jnp.bfloat16), "fsdp", axis=0, tiled=True),
        lax.all_gather(b_value.astype(jnp.bfloat16), "fsdp", axis=0, tiled=True),
        lax.all_gather(w_out.astype(jnp.bfloat16), "fsdp", axis=0, tiled=True),
        lax.all_gather(b_out.astype(jnp.bfloat16), "fsdp", axis=0, tiled=True),
    )
    gain_one, shift_one, qkv_weight, query_bias, value_bias, out_weight, out_bias = attn_full
    inputs = layer_input.astype(jnp.float32).reshape(tokens, model_width)
    normed_one, norm_back_one = jax.vjp(
        norm_layer, inputs, gain_one.astype(jnp.float32), shift_one.astype(jnp.float32)
    )
    first = normed_one.astype(jnp.bfloat16)
    qkv_bias = jnp.concatenate(
        [
            query_bias.astype(jnp.float32),
            jnp.zeros((model_width,), jnp.float32),
            value_bias.astype(jnp.float32),
        ]
    )
    qkv = (jnp.dot(first, qkv_weight, preferred_element_type=jnp.float32) + qkv_bias).astype(
        jnp.bfloat16
    )
    queries = qkv[:, :model_width].reshape(tiled)
    key_heads = qkv[:, model_width : 2 * model_width].reshape(tiled)
    value_heads = qkv[:, 2 * model_width :].reshape(tiled)
    image_segs = segments.reshape(row_count, images, PATCHES)
    matching = image_segs[:, :, :, None] == image_segs[:, :, None, :]
    occupied = (image_segs > 0)[:, :, :, None]
    diagonal = (
        lax.broadcasted_iota(jnp.int32, (PATCHES, PATCHES), 0)
        == lax.broadcasted_iota(jnp.int32, (PATCHES, PATCHES), 1)
    )[None, None]
    allowed = (matching & occupied | diagonal)[:, :, None]

    def masked_scores():
        raw = (
            jnp.einsum("rnqhe,rnkhe->rnhqk", queries, key_heads, preferred_element_type=jnp.float32)
            * scaling
        )
        return jnp.where(allowed, raw, -1000000000.0)

    scores = masked_scores()
    highest = jnp.max(scores, axis=-1, keepdims=True)
    log_total = highest + jnp.log(jnp.sum(jnp.exp(scores - highest), axis=-1, keepdims=True))
    probs_low = jnp.exp(scores - log_total).astype(jnp.bfloat16)
    context = jnp.einsum(
        "rnhqk,rnkhe->rnqhe", probs_low, value_heads, preferred_element_type=jnp.float32
    )
    context_low = context.reshape(tokens, model_width).astype(jnp.bfloat16)
    attention = jnp.dot(
        context_low, out_weight, preferred_element_type=jnp.float32
    ) + out_bias.astype(jnp.float32)
    middle = inputs + attention
    mlp_full = (
        lax.all_gather(mid_gain.astype(jnp.bfloat16), "fsdp", axis=0, tiled=True),
        lax.all_gather(mid_shift.astype(jnp.bfloat16), "fsdp", axis=0, tiled=True),
        lax.all_gather(w_up.astype(jnp.bfloat16), "fsdp", axis=0, tiled=True),
        lax.all_gather(b_up.astype(jnp.bfloat16), "fsdp", axis=0, tiled=True),
        lax.all_gather(w_down.astype(jnp.bfloat16), "fsdp", axis=0, tiled=True),
        lax.all_gather(b_down.astype(jnp.bfloat16), "fsdp", axis=0, tiled=True),
    )
    gain_two, shift_two, up_weight, up_bias, down_weight, down_bias = mlp_full
    normed_two, norm_back_two = jax.vjp(
        norm_layer, middle, gain_two.astype(jnp.float32), shift_two.astype(jnp.float32)
    )
    second = normed_two.astype(jnp.bfloat16)
    hidden = jnp.dot(second, up_weight, preferred_element_type=jnp.float32) + up_bias.astype(
        jnp.float32
    )
    activated, gelu_back = jax.vjp(gelu_exact, hidden)
    activated_low = activated.astype(jnp.bfloat16)
    branch = jnp.dot(
        activated_low, down_weight, preferred_element_type=jnp.float32
    ) + down_bias.astype(jnp.float32)
    result = (middle + branch).astype(jnp.bfloat16).reshape(row_count, slot_count, model_width)
    mlp_back = (
        lax.all_gather(mid_gain.astype(jnp.bfloat16), "fsdp", axis=0, tiled=True),
        lax.all_gather(mid_shift.astype(jnp.bfloat16), "fsdp", axis=0, tiled=True),
        lax.all_gather(w_up.astype(jnp.bfloat16), "fsdp", axis=0, tiled=True),
        lax.all_gather(b_up.astype(jnp.bfloat16), "fsdp", axis=0, tiled=True),
        lax.all_gather(w_down.astype(jnp.bfloat16), "fsdp", axis=0, tiled=True),
        lax.all_gather(b_down.astype(jnp.bfloat16), "fsdp", axis=0, tiled=True),
    )
    up_again, down_again = (mlp_back[2], mlp_back[4])
    upstream = cotangent.astype(jnp.float32).reshape(tokens, model_width)
    grad_branch = cotangent.reshape(tokens, model_width)
    grad_down = jnp.einsum(
        "tf,td->fd", activated_low, grad_branch, preferred_element_type=jnp.float32
    )
    grad_down_bias = column_sums(grad_branch)
    grad_act = jnp.einsum("td,fd->tf", grad_branch, down_again, preferred_element_type=jnp.float32)
    grad_hidden = gelu_back(grad_act)[0].astype(jnp.bfloat16)
    grad_up = jnp.einsum("td,tf->df", second, grad_hidden, preferred_element_type=jnp.float32)
    grad_up_bias = column_sums(grad_hidden)
    grad_second = jnp.einsum("tf,df->td", grad_hidden, up_again, preferred_element_type=jnp.float32)
    grad_mid_norm, grad_gain_two, grad_shift_two = norm_back_two(grad_second)
    grad_middle = upstream + grad_mid_norm
    mlp_sums = (
        lax.psum_scatter(grad_gain_two, "fsdp", scatter_dimension=0, tiled=True),
        lax.psum_scatter(grad_shift_two, "fsdp", scatter_dimension=0, tiled=True),
        lax.psum_scatter(grad_up, "fsdp", scatter_dimension=0, tiled=True),
        lax.psum_scatter(grad_up_bias, "fsdp", scatter_dimension=0, tiled=True),
        lax.psum_scatter(grad_down, "fsdp", scatter_dimension=0, tiled=True),
        lax.psum_scatter(grad_down_bias, "fsdp", scatter_dimension=0, tiled=True),
    )
    attn_back = (
        lax.all_gather(pre_gain.astype(jnp.bfloat16), "fsdp", axis=0, tiled=True),
        lax.all_gather(pre_shift.astype(jnp.bfloat16), "fsdp", axis=0, tiled=True),
        lax.all_gather(w_qkv.astype(jnp.bfloat16), "fsdp", axis=0, tiled=True),
        lax.all_gather(b_query.astype(jnp.bfloat16), "fsdp", axis=0, tiled=True),
        lax.all_gather(b_value.astype(jnp.bfloat16), "fsdp", axis=0, tiled=True),
        lax.all_gather(w_out.astype(jnp.bfloat16), "fsdp", axis=0, tiled=True),
        lax.all_gather(b_out.astype(jnp.bfloat16), "fsdp", axis=0, tiled=True),
    )
    qkv_again, out_again = (attn_back[2], attn_back[5])
    grad_attention = grad_middle.astype(jnp.bfloat16)
    grad_out = jnp.einsum(
        "ti,to->io", context_low, grad_attention, preferred_element_type=jnp.float32
    )
    grad_out_bias = column_sums(grad_attention)
    grad_context = jnp.einsum(
        "to,io->ti", grad_attention, out_again, preferred_element_type=jnp.float32
    )
    grad_context = grad_context.astype(jnp.bfloat16).reshape(tiled)
    grad_values = jnp.einsum(
        "rnhqk,rnqhe->rnkhe", probs_low, grad_context, preferred_element_type=jnp.float32
    )
    grad_probs = jnp.einsum(
        "rnqhe,rnkhe->rnhqk", grad_context, value_heads, preferred_element_type=jnp.float32
    )
    probs = jnp.exp(masked_scores() - log_total)
    grad_scores = (
        probs * (grad_probs - jnp.sum(probs * grad_probs, axis=-1, keepdims=True))
    ).astype(jnp.bfloat16)
    grad_queries = (
        jnp.einsum("rnhqk,rnkhe->rnqhe", grad_scores, key_heads, preferred_element_type=jnp.float32)
        * scaling
    )
    grad_keys = (
        jnp.einsum("rnhqk,rnqhe->rnkhe", grad_scores, queries, preferred_element_type=jnp.float32)
        * scaling
    )
    grad_qkv = jnp.concatenate(
        [
            grad_queries.reshape(tokens, model_width),
            grad_keys.reshape(tokens, model_width),
            grad_values.reshape(tokens, model_width),
        ],
        axis=1,
    ).astype(jnp.bfloat16)
    grad_qkv_weight = jnp.einsum("td,te->de", first, grad_qkv, preferred_element_type=jnp.float32)
    grad_query_bias = column_sums(grad_qkv[:, :model_width])
    grad_value_bias = column_sums(grad_qkv[:, 2 * model_width :])
    grad_first = jnp.einsum("te,de->td", grad_qkv, qkv_again, preferred_element_type=jnp.float32)
    grad_in_norm, grad_gain_one, grad_shift_one = norm_back_one(grad_first)
    grad_inputs = (
        (grad_middle + grad_in_norm)
        .astype(jnp.bfloat16)
        .reshape(row_count, slot_count, model_width)
    )
    attn_sums = (
        lax.psum_scatter(grad_gain_one, "fsdp", scatter_dimension=0, tiled=True),
        lax.psum_scatter(grad_shift_one, "fsdp", scatter_dimension=0, tiled=True),
        lax.psum_scatter(grad_qkv_weight, "fsdp", scatter_dimension=0, tiled=True),
        lax.psum_scatter(grad_query_bias, "fsdp", scatter_dimension=0, tiled=True),
        lax.psum_scatter(grad_value_bias, "fsdp", scatter_dimension=0, tiled=True),
        lax.psum_scatter(grad_out, "fsdp", scatter_dimension=0, tiled=True),
        lax.psum_scatter(grad_out_bias, "fsdp", scatter_dimension=0, tiled=True),
    )
    return (
        result,
        grad_inputs,
        attn_sums[0],
        attn_sums[1],
        attn_sums[2],
        attn_sums[3],
        attn_sums[4],
        attn_sums[5],
        attn_sums[6],
        mlp_sums[0],
        mlp_sums[1],
        mlp_sums[2],
        mlp_sums[3],
        mlp_sums[4],
        mlp_sums[5],
    )


def solution(mesh):
    return jax.shard_map(
        shards,
        mesh=mesh,
        in_specs=(
            P("fsdp", None, None),
            P("fsdp", None),
            P("fsdp", None, None),
            P("fsdp"),
            P("fsdp"),
            P("fsdp", None),
            P("fsdp"),
            P("fsdp"),
            P("fsdp", None),
            P("fsdp"),
            P("fsdp"),
            P("fsdp"),
            P("fsdp", None),
            P("fsdp"),
            P("fsdp", None),
            P("fsdp"),
        ),
        out_specs=(
            P("fsdp", None, None),
            P("fsdp", None, None),
            P("fsdp"),
            P("fsdp"),
            P("fsdp", None),
            P("fsdp"),
            P("fsdp"),
            P("fsdp", None),
            P("fsdp"),
            P("fsdp"),
            P("fsdp"),
            P("fsdp", None),
            P("fsdp"),
            P("fsdp", None),
            P("fsdp"),
        ),
        check_vma=False,
    )
```

profile of v0, /device:TPU:0, one launch (start us, length us, event | category | flops | bytes accessed | tf_op | source)
XLA Modules:
  0.0 820.7 jit_solution(5012870485716930246)
XLA Ops:
  7.2 1.7 convert_element_type.139
  9.0 1.5 convert_element_type.149
  10.6 1.6 convert_element_type.157
  12.3 1.6 convert_element_type.161
  14.0 0.7 convert_element_type.134
  14.7 0.7 convert_element_type.136
  19.9 1.6 convert_reduce_fusion.4
  24.2 43.6 %all-reduce.19 = (bf16[768]{0:T(1024)(128)(2,1)S(1)}, bf16[768]{0:T(1024)(128)(2,1)S(1)}, bf16[768]{0:T(1024)(128)(2,1)S(1)}, bf16[768]{0:T(1024)(128)(2,1)S(1)}...) all-reduce(bf16[768]{0:T(1024)(128)(2,1)S(1)} %dynamic-update-slice, ...), channel_id=1, replica_groups=mesh['fsdp'=32] {'fsdp'}, use_global_device_ids=true, to_apply=%add.1 | all-reduce | flops 9216 | bytes 36864
  68.6 0.9 and_or_fusion
  70.1 4.4 all-gather.5.cloned.1.call-done
  74.5 5.5 add_convert_fusion.1
  80.0 1.3 fusion.35
  81.3 3.5 reshape.188
  84.8 3.5 reshape.189
  88.3 4.1 reshape.187
  92.4 6.7 fusion.6
  99.1 2.3 exponential_reduce_fusion
  101.4 2.3 convert_bitcast_fusion.1
  103.8 0.8 copy.59
  104.6 3.4 convert_element_type.148
  108.0 22.8 %all-gather.7.cloned.1.call-done = bf16[768,768]{1,0:T(8,128)(2,1)} async-done(((bf16[24,768]{1,0:T(8,128)(2,1)}), bf16[768,768]{1,0:T(8,128)(2,1)}) %all-gather.7.cloned.1.call-update) | async-done | bytes 1179664 | tf_op jit(solution)/shard_map/all_gather | solution.py:56
  130.8 3.4 fusion.36
  134.7 0.9 copy-done.36
  135.6 61.3 %all-gather.9.cloned.1.call-done = bf16[768,3072]{1,0:T(8,128)(2,1)} async-done(((bf16[24,3072]{1,0:T(8,128)(2,1)}), bf16[768,3072]{1,0:T(8,128)(2,1)}) %all-gather.9.cloned.1.call-update) | async-done | bytes 4718608 | tf_op jit(solution)/shard_map/all_gather | solution.py:109
  196.9 9.4 %fusion.31 = f32[864,3072]{1,0:T(8,128)} fusion(bf16[768,3072]{1,0:T(8,128)(2,1)} %all-gather.9.cloned.1.call-done, f32[864,768]{1,0:T(8,128)S(1)} %get-tuple-element.52, f32[768]{0:T(1024)S(1)} %convert_element_type.155, f32[768]{0:T(1024)S(1)} %convert_element_type.153, f32[864]{0:T(1024)S(1)} %fusion.27, f32[864]{0:T(1024)S(1)} %broadcast_multiply_fusion.1), kind=kOutput, calls=%fused_computation.83 | convolution fusion | flops 4080181248 | bytes 18002688 | tf_op jit(solution)/shard_map/dot_general | solution.py:119
  206.3 55.8 %all-gather.11.cloned.1.call-done = bf16[3072,768]{1,0:T(8,128)(2,1)} async-done(((bf16[96,768]{1,0:T(8,128)(2,1)}), bf16[3072,768]{1,0:T(8,128)(2,1)}) %all-gather.11.cloned.1.call-update) | async-done | bytes 4718608 | tf_op jit(solution)/shard_map/all_gather | solution.py:111
  262.1 33.5 %convert_reduce_fusion = (f32[3072]{0:T(1024)}, bf16[864,3072]{1,0:T(8,128)(2,1)S(1)}, f32[864,3072]{1,0:T(8,128)}) fusion(f32[864,3072]{1,0:T(8,128)} %fusion.31, f32[3072]{0:T(1024)S(1)} %copy-done.28, bf16[864,768]{1,0:T(8,128)(2,1)} %bitcast.51, bf16[3072,768]{1,0:T(8,128)(2,1)} %all-gather.11.cloned.1.call-done), kind=kOutput, calls=%fused_computation.2 | convolution fusion | flops 4275926016 | bytes 32612352 | tf_op jit(solution)/shard_map/td,fd->tf/dot_general | solution.py:143
  295.6 5.3 multiply_reduce_fusion.1
  301.0 1.0 fusion.34
  302.0 1.6 copy-done.7
  303.6 1.1 convert_reduce_fusion.1
  304.6 2.9 fusion.38
  307.6 2.5 convolution_convert_fusion
  310.2 3.7 reshape.193
  313.9 8.1 multiply_reduce_fusion
  322.0 2.1 multiply_convert_fusion.3
  324.1 2.0 fusion.8
  326.2 2.6 copy.64
  328.7 5.7 reshape.194
  334.4 3.7 fusion.9
  338.2 2.6 copy.66
  340.8 5.9 reshape.195
  346.7 4.5 convert_bitcast_fusion
  351.1 0.8 copy.68
  352.0 3.0 reshape.196
  355.0 1.6 constant_dynamic-update-slice_fusion.2
  357.2 1.9 copy-done.25
  359.1 5.9 fusion.37
  365.0 1.7 copy-done.2
  366.8 10.3 %fusion.30 = f32[768,3072]{1,0:T(8,128)} fusion(bf16[864,3072]{1,0:T(8,128)(2,1)} %copy-done.15, f32[864,768]{1,0:T(8,128)S(1)} %copy-done.2, f32[768]{0:T(1024)S(1)} %copy-done.27, f32[768]{0:T(1024)S(1)} %convert_element_type.153, f32[864]{0:T(1024)S(1)} %fusion.27, f32[864]{0:T(1024)S(1)} %broadcast_multiply_fusion.1), kind=kOutput, calls=%fused_computation.82 | convolution fusion | flops 4080181248 | bytes 17412864 | tf_op jit(solution)/shard_map/td,tf->df/dot_general | solution.py:145
  377.7 8.8 %multiply_convert_fusion = bf16[864,3072]{1,0:T(8,128)(2,1)S(1)} fusion(f32[864,3072]{1,0:T(8,128)} %get-tuple-element.41, f32[864,3072]{1,0:T(8,128)} %fusion.31, f32[3072]{0:T(1024)S(1)} %copy-done.29), kind=kLoop, calls=%fused_computation.4 | loop fusion | flops 10616832 | bytes 26554368 | tf_op jit(solution)/shard_map/convert_element_type | solution.py:123
  386.5 2.4 copy-done.16
  389.0 7.7 fusion.39
  397.3 1.7 convert_reduce_fusion.5
  399.0 1.6 convert_reduce_fusion.3
  400.9 8.4 %multiply_reduce_fusion.2 = (f32[768]{0:T(1024)S(1)}, f32[864]{0:T(1024)S(1)}, f32[768]{0:T(1024)S(1)}, f32[864,768]{1,0:T(8,128)}) fusion(f32[864]{0:T(1024)S(1)} %copy-done.33, f32[864]{0:T(1024)S(1)} %copy-done.31, bf16[3,288,768]{2,1,0:T(8,128)(2,1)S(1)} %copy-done.9, f32[768]{0:T(1024)S(1)} %copy-done.35, bf16[864,2304]{1,0:T(8,128)(2,1)} %copy-done.25, ...), kind=kOutput, calls=%fused_computation.39 | convolution fusion | flops 3064944384 | bytes 12848256 | tf_op jit(solution)/shard_map/te,de->td/dot_general | solution.py:206
  409.3 40.5 %all-reduce.18 = (f32[768]{0:T(1024)S(1)}, f32[768]{0:T(1024)S(1)}, f32[768]{0:T(1024)S(1)}, f32[768]{0:T(1024)S(1)}, f32[768]{0:T(1024)S(1)}, /*index=5*/f32[76...) all-reduce(f32[768]{0:T(1024)S(1)} %get-tuple-element.17, ...), channel_id=2, replica_groups=mesh['fsdp'=32] {'fsdp'}, use_global_device_ids=true, to_apply=%region_12.13.clone | all-reduce | flops 9216 | bytes 73728
  454.5 4.3 add_add_fusion
  458.8 2.0 reduce_sum.182
  461.3 5.4 add_convert_fusion.2
  466.7 9.3 %add_convert_fusion.3 = bf16[864,768]{1,0:T(8,128)(2,1)} fusion(f32[864,768]{1,0:T(8,128)S(1)} %copy-done.2, bf16[864,3072]{1,0:T(8,128)(2,1)} %copy-done.16, bf16[3072,768]{1,0:T(8,128)(2,1)} %all-gather.11.cloned.1.call-done, f32[768]{0:T(1024)S(1)} %convert_element_type.163), kind=kOutput, calls=%fused_computation.43 | convolution fusion | flops 4078854144 | bytes 14011392 | tf_op jit(solution)/shard_map/dot_general | solution.py:124
  476.0 54.4 %reduce-scatter.5.cloned.1.call-done = f32[24,2304]{1,0:T(8,128)} async-done(((f32[768,2304]{1,0:T(8,128)}), f32[24,2304]{1,0:T(8,128)}) %reduce-scatter.5.cloned.1.call-update) | async-done | bytes 221200 | tf_op jit(solution)/shard_map/reduce_scatter | solution.py:216
  530.4 141.6 %reduce-scatter.9.cloned.1.call-done = f32[24,3072]{1,0:T(8,128)} async-done(((f32[768,3072]{1,0:T(8,128)}), f32[24,3072]{1,0:T(8,128)}) %reduce-scatter.9.cloned.1.call-update) | async-done | bytes 294928 | tf_op jit(solution)/shard_map/reduce_scatter | solution.py:153
  671.9 141.6 %reduce-scatter.11.cloned.1.call-done = f32[96,768]{1,0:T(8,128)} async-done(((f32[3072,768]{1,0:T(8,128)}), f32[96,768]{1,0:T(8,128)}) %reduce-scatter.11.cloned.1.call-update) | async-done | bytes 294928 | tf_op jit(solution)/shard_map/reduce_scatter | solution.py:155
  (177 shorter events, 17.0 us)
Async XLA Ops:
  7.2 14.5 %copy-start.8 = (bf16[3,288,768]{2,1,0:T(8,128)(2,1)S(1)}, bf16[3,288,768]{2,1,0:T(8,128)(2,1)}, u32[]{:S(2)}) copy-start(bf16[3,288,768]{2,1,0:T(8,128)(2,1)} %param.16) | copy-start | bytes 3981316
  7.2 61.3 %copy-start.42 = (s32[3,288]{1,0:T(4,128)S(1)}, s32[3,288]{1,0:T(4,128)}, u32[]{:S(2)}) copy-start(s32[3,288]{1,0:T(4,128)} %param.17) | copy-start | bytes 10372
  7.2 67.3 %all-gather.5.cloned.1.call-start = ((), (), s32[]{:S(2)}) async-start(), calls=%async_computation.4 | async-start | bytes 3649536 | tf_op jit(solution)/shard_map/all_gather | solution.py:53
  9.0 121.9 %all-gather.7.cloned.1.call-start = ((), (), s32[]{:S(2)}) async-start(), calls=%async_computation.5 | async-start | bytes 1216512 | tf_op jit(solution)/shard_map/all_gather | solution.py:56
  10.5 186.3 %all-gather.9.cloned.1.call-start = ((), (), s32[]{:S(2)}) async-start(), calls=%async_computation.6 | async-start | bytes 4866048 | tf_op jit(solution)/shard_map/all_gather | solution.py:109
  12.3 249.9 %all-gather.11.cloned.1.call-start = ((), (), s32[]{:S(2)}) async-start(), calls=%async_computation.7 | async-start | bytes 4866048 | tf_op jit(solution)/shard_map/all_gather | solution.py:111
  14.0 462.0 %reduce-scatter.7.cloned.1.call-start = ((), (), s32[]{:S(2)}) async-start(), calls=%async_computation.9 | async-start | bytes 2433024 | tf_op jit(solution)/shard_map/reduce_scatter | solution.py:219
  21.6 58.3 %copy-start.30 = (f32[864]{0:T(1024)}, f32[864]{0:T(1024)S(1)}, u32[]{:S(2)}) copy-start(f32[864]{0:T(1024)S(1)} %div.39) | copy-start | bytes 10372
  22.3 45.6 %copy-start.38 = (f32[864]{0:T(1024)}, f32[864]{0:T(1024)S(1)}, u32[]{:S(2)}) copy-start(f32[864]{0:T(1024)S(1)} %add.118) | copy-start | bytes 10372
  22.3 57.7 %copy-start.32 = (f32[864]{0:T(1024)}, f32[864]{0:T(1024)S(1)}, u32[]{:S(2)}) copy-start(f32[864]{0:T(1024)S(1)} %rsqrt.20) | copy-start | bytes 10372
  67.8 12.1 %copy-start.34 = (f32[768]{0:T(1024)}, f32[768]{0:T(1024)S(1)}, u32[]{:S(2)}) copy-start(f32[768]{0:T(1024)S(1)} %convert_element_type.135) | copy-start | bytes 9220
  67.9 129.0 %copy-start.26 = (f32[768]{0:T(1024)}, f32[768]{0:T(1024)S(1)}, u32[]{:S(2)}) copy-start(f32[768]{0:T(1024)S(1)} %convert_element_type.155) | copy-start | bytes 9220
  70.0 4.4 copy-start.22
  92.4 9.0 %copy-start.5 = (bf16[3,8,36,12,64]{4,3,2,1,0:T(8,128)(2,1)}, bf16[3,8,36,12,64]{4,3,2,1,0:T(8,128)(2,1)S(1)}, u32[]{:S(2)}) copy-start(bf16[3,8,36,12,64]{4,3,2,1,0:T(8,128)(2,1)S(1)} %reshape.187) | copy-start | bytes 3981316
  92.4 6.7 copy-start.20
  99.1 4.7 copy-start
  101.4 2.4 copy-start.18
  134.2 166.7 %copy-start.1 = (f32[864,768]{1,0:T(8,128)}, f32[864,768]{1,0:T(8,128)S(1)}, u32[]{:S(2)}) copy-start(f32[864,768]{1,0:T(8,128)S(1)} %get-tuple-element.52) | copy-start | bytes 7962628
  134.7 0.9 copy-start.36
  135.6 126.5 %copy-start.28 = (f32[3072]{0:T(1024)S(1)}, f32[3072]{0:T(1024)}, u32[]{:S(2)}) copy-start(f32[3072]{0:T(1024)} %convert_element_type.159) | copy-start | bytes 36868
  262.1 33.5 %copy-start.46 = (bf16[768,3072]{1,0:T(8,128)(2,1)S(1)}, bf16[768,3072]{1,0:T(8,128)(2,1)}, u32[]{:S(2)}) copy-start(bf16[768,3072]{1,0:T(8,128)(2,1)} %all-gather.9.cloned.1.call-done) | copy-start | bytes 14155780
  295.6 5.3 copy-start.15
  295.6 5.3 copy-start.37
  301.0 2.6 copy-start.10
  302.0 1.6 copy-start.7
  302.0 2.7 copy-start.24
  307.6 222.8 %reduce-scatter.5.cloned.1.call-start = ((), (), s32[]{:S(2)}) async-start(), calls=%async_computation.8 | async-start | bytes 7299072 | tf_op jit(solution)/shard_map/reduce_scatter | solution.py:216
  310.1 3.7 copy-start.19
  310.1 3.7 copy-start.21
  310.2 11.8 %slice-start = ((s8[5898240]{0:T(1024)(128)(4,1)}), s8[1703936]{0:T(1024)(128)(4,1)S(1)}, s32[]{:S(2)}) async-start(s8[5898240]{0:T(1024)(128)(4,1)} %bitcast.47), calls=%async_computation.12 | async-start | bytes 3407872
  313.8 8.1 slice-start.1
  322.0 2.2 copy-start.14
  324.1 2.0 copy-start.3
  328.7 5.7 copy-start.4
  340.8 5.9 copy-start.6
  355.0 1.7 copy-start.17
  355.0 2.1 copy-start.12
  355.0 4.1 copy-start.23
  357.2 1.9 copy-start.25
  365.0 1.8 copy-start.2
  365.0 1.8 copy-start.27
  365.0 306.9 %reduce-scatter.9.cloned.1.call-start = ((), (), s32[]{:S(2)}) async-start(), calls=%async_computation.10 | async-start | bytes 9732096 | tf_op jit(solution)/shard_map/reduce_scatter | solution.py:153
  377.0 0.7 copy-start.29
  377.1 436.5 %reduce-scatter.11.cloned.1.call-start = ((), (), s32[]{:S(2)}) async-start(), calls=%async_computation.11 | async-start | bytes 9732096 | tf_op jit(solution)/shard_map/reduce_scatter | solution.py:155
  377.7 11.2 %copy-start.11 = (bf16[3,288,768]{2,1,0:T(8,128)(2,1)S(1)}, bf16[3,288,768]{2,1,0:T(8,128)(2,1)}, u32[]{:S(2)}) copy-start(bf16[3,288,768]{2,1,0:T(8,128)(2,1)} %param.18) | copy-start | bytes 3981316
  386.5 2.4 copy-start.16
  396.6 0.7 copy-start.45
  396.7 4.2 copy-start.31
  396.7 4.2 copy-start.33
  396.7 4.2 copy-start.35
  396.7 3.9 copy-start.13
  396.7 4.1 copy-start.9
  400.9 8.5 %copy-start.40 = (f32[768]{0:T(1024)S(1)}, f32[768]{0:T(1024)}, u32[]{:S(2)}) copy-start(f32[768]{0:T(1024)} %get-tuple-element.42) | copy-start | bytes 9220
  400.9 8.4 %copy-start.41 = (f32[3072]{0:T(1024)S(1)}, f32[3072]{0:T(1024)}, u32[]{:S(2)}) copy-start(f32[3072]{0:T(1024)} %get-tuple-element.39) | copy-start | bytes 36868
  400.9 8.4 %copy-start.43 = (f32[768]{0:T(1024)S(1)}, f32[768]{0:T(1024)}, u32[]{:S(2)}) copy-start(f32[768]{0:T(1024)} %get-tuple-element.15) | copy-start | bytes 9220
  400.9 8.4 %copy-start.44 = (f32[768]{0:T(1024)S(1)}, f32[768]{0:T(1024)}, u32[]{:S(2)}) copy-start(f32[768]{0:T(1024)} %get-tuple-element.19) | copy-start | bytes 9220
  400.9 53.6 %copy-start.39 = (f32[864]{0:T(1024)S(1)}, f32[864]{0:T(1024)}, u32[]{:S(2)}) copy-start(f32[864]{0:T(1024)} %copy-done.38) | copy-start | bytes 10372
Sparse Core Ops, SparseCore 0:
  11.5 62.9 all-gather.4
  78.0 52.8 all-gather.6
  134.3 62.4 all-gather.8
  200.2 61.9 all-gather.10
  307.7 97.9 reduce-scatter.6
  411.8 118.5 reduce-scatter.4
  536.8 135.0 reduce-scatter.8
  678.4 135.1 reduce-scatter.10
where the time goes:
time: 825 us; the launch traced here: 821 us
  waiting for transfers between devices  482 us (58%)
  matrix products  131 us (16%)
  blocking collectives  84.1 us (10%)
  local copies, waits for them, and re-layouts  60.3 us (7%)
  other arithmetic  47.5 us (6%)
  between operations  15.2 us (2%)
    reduce_scatter x1, waiting for transfers between devices, shards(): lax.psum_scatter(grad_down, 'fsdp', scatter_dimension=0, tiled=True)  142 us
    reduce_scatter x1, waiting for transfers between devices, shards(): lax.psum_scatter(grad_up, 'fsdp', scatter_dimension=0, tiled=True)  142 us
    unnamed x2, blocking collectives  84.1 us
    all_gather x1, waiting for transfers between devices, shards(): lax.all_gather(w_up.astype(jnp.bfloat16), 'fsdp', axis=0, tiled=True)  61.3 us
    all_gather x1, waiting for transfers between devices, shards(): lax.all_gather(w_down.astype(jnp.bfloat16), 'fsdp', axis=0, tiled=True)  55.8 us
    reduce_scatter x1, waiting for transfers between devices, shards(): lax.psum_scatter(grad_qkv_weight, 'fsdp', scatter_dimension=0, tiled=True)  54.4 us
    dot_general x1, matrix products, shards(): jnp.einsum('td,fd->tf', grad_branch, down_again, preferred_element_type=j...  33.5 us
    all_gather x1, waiting for transfers between devices, shards(): lax.all_gather(w_out.astype(jnp.bfloat16), 'fsdp', axis=0, tiled=True)  22.8 us
  transfers between devices with their start and end apart: 8, of which 7 were waited for; matrix products, arithmetic and copies ran while one was open for 22% of the time, Pallas kernels for 0%

commit v1 on v0

--- a/solution.py
+++ b/solution.py
@@ -1,3 +1,4 @@
+import functools
 import jax
 import jax.numpy as jnp
 from jax import lax
@@ -6,6 +7,35 @@
 HEAD_DIM = 64
 PATCHES = 36
 EPSILON = 1e-06
+
+
+def apply_modes(xx, which_dim):
+    a_now = list(xx.shape[1:])
+    a_now[which_dim] *= xx.shape[0]
+    return jnp.moveaxis(xx, 0, which_dim).reshape(a_now)
+
+
+def _store_lanes(z, device_axis):
+    n_now = jax.lax.axis_size(device_axis)
+    oldest, r2 = (n_now, jax.lax.axis_index(device_axis))
+    o_now, value_now = (z[None], 1)
+    while value_now < oldest:
+        spare = jax.lax.ppermute(
+            o_now, device_axis, tuple(((k, k ^ value_now) for k in range(oldest)))
+        )
+        top = r2 & value_now == 0
+        even = jnp.where(top, o_now, spare)
+        o_now = jnp.concatenate([even, jnp.where(top, spare, o_now)])
+        value_now *= 2
+    return o_now
+
+
+def quarters_take(local_values, local_block, axis_k):
+    placed = _store_lanes(local_values, local_block)
+    return apply_modes(placed, axis_k)
+
+
+define_tails = functools.partial(quarters_take, local_block="fsdp", axis_k=0)
 
 
 def norm_layer(value, gain, shift):
@@ -108,7 +138,7 @@
         lax.all_gather(mid_shift.astype(jnp.bfloat16), "fsdp", axis=0, tiled=True),
         lax.all_gather(w_up.astype(jnp.bfloat16), "fsdp", axis=0, tiled=True),
         lax.all_gather(b_up.astype(jnp.bfloat16), "fsdp", axis=0, tiled=True),
-        lax.all_gather(w_down.astype(jnp.bfloat16), "fsdp", axis=0, tiled=True),
+        define_tails(w_down.astype(jnp.bfloat16)),
         lax.all_gather(b_down.astype(jnp.bfloat16), "fsdp", axis=0, tiled=True),
     )
     gain_two, shift_two, up_weight, up_bias, down_weight, down_bias = mlp_full

time: 825 us -> 920 us (1.12)
  waiting for transfers between devices: 482 us -> 543 us
  other arithmetic: 47.5 us -> 62.1 us
  local copies, waits for them, and re-layouts: 60.3 us -> 73.7 us
    ppermute x0 -> x5, waiting for transfers between devices: none -> 175 us  [_store_lanes(): jax.lax.ppermute(o_now, device_axis, tuple(((k, k ^ value_now) for k in r...]
    reduce_scatter x1, waiting for transfers between devices: 142 us -> 83.9 us  [shards(): lax.psum_scatter(grad_up, 'fsdp', scatter_dimension=0, tiled=True)]
    reduce_scatter x1, waiting for transfers between devices: 54.4 us -> 0.01 us  [shards(): lax.psum_scatter(grad_qkv_weight, 'fsdp', scatter_dimension=0, tiled=True)]
    unnamed x127 -> x123, local copies, waits for them, and re-layouts: 19.2 us -> 22.9 us
  transfers between devices with their start and end apart: 8 -> 13, of which waited for: 7 -> 11; matrix products, arithmetic and copies ran while one was open for 22% -> 21% of each run, Pallas kernels for 0% -> 0%
where the time goes in v1:
time: 920 us; the launch traced here: 916 us
  waiting for transfers between devices  543 us (59%)
  matrix products  132 us (14%)
  blocking collectives  82.5 us (9%)
  local copies, waits for them, and re-layouts  73.7 us (8%)
  other arithmetic  62.1 us (7%)
  between operations  15 us (2%)
    ppermute x5, waiting for transfers between devices, _store_lanes(): jax.lax.ppermute(o_now, device_axis, tuple(((k, k ^ value_now) for k in r...  175 us
    reduce_scatter x1, waiting for transfers between devices, shards(): lax.psum_scatter(grad_down, 'fsdp', scatter_dimension=0, tiled=True)  142 us
    reduce_scatter x1, waiting for transfers between devices, shards(): lax.psum_scatter(grad_up, 'fsdp', scatter_dimension=0, tiled=True)  83.9 us
    unnamed x2, blocking collectives  82.5 us
    all_gather x1, waiting for transfers between devices, shards(): lax.all_gather(w_up.astype(jnp.bfloat16), 'fsdp', axis=0, tiled=True)  62.1 us
    all_gather x1, waiting for transfers between devices, shards(): lax.all_gather(w_down.astype(jnp.bfloat16), 'fsdp', axis=0, tiled=True)  55.8 us
    dot_general x1, matrix products, shards(): jnp.einsum('td,fd->tf', grad_branch, down_again, preferred_element_type=j...  33.8 us
    unnamed x123, local copies, waits for them, and re-layouts  22.9 us
  transfers between devices with their start and end apart: 13, of which 11 were waited for; matrix products, arithmetic and copies ran while one was open for 21% of the time, Pallas kernels for 0%

profile of v1, /device:TPU:0, one launch (start us, length us, event | category | flops | bytes accessed | tf_op | source)
XLA Modules:
  0.0 915.5 jit_solution(4699305314801459004)
XLA Ops:
  7.2 1.7 convert_element_type.139
  9.0 1.5 convert_element_type.149
  10.6 1.6 convert_element_type.157
  12.3 1.6 convert_element_type.161
  21.8 43.3 %all-reduce.19 = (bf16[768]{0:T(1024)(128)(2,1)S(1)}, bf16[768]{0:T(1024)(128)(2,1)S(1)}, bf16[768]{0:T(1024)(128)(2,1)S(1)}, bf16[768]{0:T(1024)(128)(2,1)S(1)}...) all-reduce(bf16[768]{0:T(1024)(128)(2,1)S(1)} %dynamic-update-slice, ...), channel_id=1, replica_groups=mesh['fsdp'=32] {'fsdp'}, use_global_device_ids=true, to_apply=%add.1 | all-reduce | flops 9216 | bytes 36864
  65.1 1.6 convert_reduce_fusion.4
  70.2 4.6 all-gather.5.cloned.1.call-done
  74.8 5.5 add_convert_fusion.1
  80.3 2.1 fusion.35
  82.4 4.1 reshape.190
  86.5 5.5 reshape.192
  92.0 5.2 reshape.191
  97.2 5.4 fusion.6
  102.7 2.3 exponential_reduce_fusion
  105.2 2.5 convert_bitcast_fusion.1
  108.6 3.0 convert_element_type.148
  111.6 19.5 %all-gather.7.cloned.1.call-done = bf16[768,768]{1,0:T(8,128)(2,1)} async-done(((bf16[24,768]{1,0:T(8,128)(2,1)}), bf16[768,768]{1,0:T(8,128)(2,1)}) %all-gather.7.cloned.1.call-update) | async-done | bytes 1179664 | tf_op jit(solution)/shard_map/all_gather | solution.py:86
  131.0 3.4 fusion.36
  134.9 62.1 %all-gather.9.cloned.1.call-done = bf16[768,3072]{1,0:T(8,128)(2,1)} async-done(((bf16[24,3072]{1,0:T(8,128)(2,1)}), bf16[768,3072]{1,0:T(8,128)(2,1)}) %all-gather.9.cloned.1.call-update) | async-done | bytes 4718608 | tf_op jit(solution)/shard_map/all_gather | solution.py:139
  197.0 9.5 %fusion.31 = f32[864,3072]{1,0:T(8,128)} fusion(bf16[768,3072]{1,0:T(8,128)(2,1)} %all-gather.9.cloned.1.call-done, f32[864,768]{1,0:T(8,128)S(1)} %get-tuple-element.62, f32[768]{0:T(1024)S(1)} %convert_element_type.155, f32[768]{0:T(1024)S(1)} %convert_element_type.153, f32[864]{0:T(1024)S(1)} %fusion.27, f32[864]{0:T(1024)S(1)} %broadcast_multiply_fusion.1), kind=kOutput, calls=%fused_computation.98 | convolution fusion | flops 4080181248 | bytes 18002688 | tf_op jit(solution)/shard_map/dot_general | solution.py:149
  206.5 55.8 %all-gather.11.cloned.1.call-done = bf16[3072,768]{1,0:T(8,128)(2,1)} async-done(((bf16[96,768]{1,0:T(8,128)(2,1)}), bf16[3072,768]{1,0:T(8,128)(2,1)}) %all-gather.11.cloned.1.call-update) | async-done | bytes 4718608 | tf_op jit(solution)/shard_map/all_gather | solution.py:163
  262.3 33.8 %convert_reduce_fusion = (f32[3072]{0:T(1024)}, bf16[864,3072]{1,0:T(8,128)(2,1)S(1)}, f32[864,3072]{1,0:T(8,128)}) fusion(f32[864,3072]{1,0:T(8,128)} %fusion.31, f32[3072]{0:T(1024)S(1)} %copy-done.30, bf16[864,768]{1,0:T(8,128)(2,1)} %bitcast.54, bf16[3072,768]{1,0:T(8,128)(2,1)} %all-gather.11.cloned.1.call-done), kind=kOutput, calls=%fused_computation.2 | convolution fusion | flops 4275926016 | bytes 32612352 | tf_op jit(solution)/shard_map/td,fd->tf/dot_general | solution.py:173
  296.2 5.3 multiply_reduce_fusion.1
  305.6 2.8 fusion.38
  308.4 4.0 convolution_convert_fusion
  312.3 5.3 reshape.197
  317.6 10.2 %multiply_reduce_fusion = (f32[3,8,12,36]{3,2,1,0:T(8,128)S(1)}, f32[3,8,12,36,36]{3,4,2,1,0:T(8,128)}) fusion(f32[3,8,12,36,36]{3,4,2,1,0:T(8,128)} %copy-done, f32[3,8,12,36]{3,2,1,0:T(8,128)S(1)} %copy-done.17, pred[3,8,36,36]{2,3,1,0:T(8,128)(4,1)S(1)} %copy-done.19, bf16[3,8,36,12,64]{4,3,2,1,0:T(8,128)(2,1)} %copy-done.2, ...), kind=kOutput, calls=%fused_computation.22 | convolution fusion | flops 49631616 | bytes 5754240 | tf_op jit(solution)/shard_map/rnqhe,rnkhe->rnhqk/dot_general | solution.py:210
  327.9 5.9 multiply_convert_fusion.3
  333.8 2.0 fusion.8
  335.8 2.7 copy.64
  338.5 5.5 reshape.198
  344.1 4.7 fusion.9
  348.7 2.6 copy.66
  351.3 5.5 reshape.199
  356.9 5.5 convert_bitcast_fusion
  362.4 2.6 copy.68
  365.1 5.5 reshape.200
  370.6 1.6 constant_dynamic-update-slice_fusion.2
  372.8 2.0 copy-done.26
  374.8 6.0 fusion.37
  381.4 10.6 %fusion.30 = f32[768,3072]{1,0:T(8,128)} fusion(bf16[864,3072]{1,0:T(8,128)(2,1)} %copy-done.12, f32[864,768]{1,0:T(8,128)S(1)} %get-tuple-element.62, f32[768]{0:T(1024)S(1)} %copy-done.29, f32[768]{0:T(1024)S(1)} %convert_element_type.153, f32[864]{0:T(1024)S(1)} %fusion.27, f32[864]{0:T(1024)S(1)} %broadcast_multiply_fusion.1), kind=kOutput, calls=%fused_computation.97 | convolution fusion | flops 4080181248 | bytes 17412864 | tf_op jit(solution)/shard_map/td,tf->df/dot_general | solution.py:175
  392.1 8.6 multiply_convert_fusion
  400.7 2.4 copy-done.14
  403.1 7.7 fusion.39
  414.8 7.9 collective-permute-done.1
  426.1 13.5 %collective-permute-done.2 = bf16[4,96,768]{2,1,0:T(8,128)(2,1)} collective-permute-done((bf16[4,96,768]{2,1,0:T(8,128)(2,1)}, bf16[4,96,768]{2,1,0:T(8,128)(2,1)}, u32[]{:S(2)}, u32[]{:S(2)}) %collective-permute-start.2) | collective-permute-done | bytes 589856 | tf_op jit(solution)/shard_map/ppermute | solution.py:23
  444.2 25.4 %collective-permute-done.3 = bf16[8,96,768]{2,1,0:T(8,128)(2,1)} collective-permute-done((bf16[8,96,768]{2,1,0:T(8,128)(2,1)}, bf16[8,96,768]{2,1,0:T(8,128)(2,1)}, u32[]{:S(2)}, u32[]{:S(2)}) %collective-permute-start.3) | collective-permute-done | bytes 1179680 | tf_op jit(solution)/shard_map/ppermute | solution.py:23
  469.6 1.6 broadcast_select_fusion.3
  472.2 1.6 pad_maximum_fusion.1
  473.9 1.9 collective-permute-start.4
  475.7 1.6 convert_reduce_fusion.5
  477.3 127.7 %collective-permute-done.4 = bf16[16,96,768]{2,1,0:T(8,128)(2,1)} collective-permute-done((bf16[16,96,768]{2,1,0:T(8,128)(2,1)}, bf16[16,96,768]{2,1,0:T(8,128)(2,1)}, u32[]{:S(2)}, u32[]{:S(2)}) %collective-permute-start.4) | collective-permute-done | bytes 2359328 | tf_op jit(solution)/shard_map/ppermute | solution.py:23
  605.0 2.6 broadcast_select_fusion.1
  607.7 2.8 pad_maximum_fusion
  613.0 3.9 multiply_reduce_fusion.2
  616.9 2.2 add_add_fusion
  619.1 2.0 reduce_sum.182
  621.1 1.6 convert_reduce_fusion.3
  622.7 1.6 convert_reduce_fusion.2
  624.3 39.3 %all-reduce.18 = (f32[768]{0:T(1024)S(1)}, f32[768]{0:T(1024)S(1)}, f32[768]{0:T(1024)S(1)}, f32[768]{0:T(1024)S(1)}, f32[768]{0:T(1024)S(1)}, /*index=5*/f32[76...) all-reduce(f32[768]{0:T(1024)S(1)} %get-tuple-element.17, ...), channel_id=2, replica_groups=mesh['fsdp'=32] {'fsdp'}, use_global_device_ids=true, to_apply=%region_12.13.clone | all-reduce | flops 9216 | bytes 73728
  668.8 4.8 add_convert_fusion.2
  673.6 9.3 %add_convert_fusion.3 = bf16[864,768]{1,0:T(8,128)(2,1)} fusion(f32[864,768]{1,0:T(8,128)S(1)} %get-tuple-element.62, bf16[864,3072]{1,0:T(8,128)(2,1)} %copy-done.14, bf16[3072,768]{1,0:T(8,128)(2,1)} %bitcast.56, f32[768]{0:T(1024)S(1)} %convert_element_type.163), kind=kOutput, calls=%fused_computation.44 | convolution fusion | flops 4078854144 | bytes 14011392 | tf_op jit(solution)/shard_map/dot_general | solution.py:154
  682.9 83.9 %reduce-scatter.9.cloned.1.call-done = f32[24,3072]{1,0:T(8,128)} async-done(((f32[768,3072]{1,0:T(8,128)}), f32[24,3072]{1,0:T(8,128)}) %reduce-scatter.9.cloned.1.call-update) | async-done | bytes 294928 | tf_op jit(solution)/shard_map/reduce_scatter | solution.py:183
  766.8 141.7 %reduce-scatter.11.cloned.1.call-done = f32[96,768]{1,0:T(8,128)} async-done(((f32[3072,768]{1,0:T(8,128)}), f32[96,768]{1,0:T(8,128)}) %reduce-scatter.11.cloned.1.call-update) | async-done | bytes 294928 | tf_op jit(solution)/shard_map/reduce_scatter | solution.py:185
  (193 shorter events, 39.2 us)
Async XLA Ops:
  7.2 59.6 %copy-start.4 = (bf16[3,288,768]{2,1,0:T(8,128)(2,1)S(1)}, bf16[3,288,768]{2,1,0:T(8,128)(2,1)}, u32[]{:S(2)}) copy-start(bf16[3,288,768]{2,1,0:T(8,128)(2,1)} %param.16) | copy-start | bytes 3981316
  7.2 60.8 %copy-start.42 = (s32[3,288]{1,0:T(4,128)S(1)}, s32[3,288]{1,0:T(4,128)}, u32[]{:S(2)}) copy-start(s32[3,288]{1,0:T(4,128)} %param.17) | copy-start | bytes 10372
  7.2 67.6 %all-gather.5.cloned.1.call-start = ((), (), s32[]{:S(2)}) async-start(), calls=%async_computation.4 | async-start | bytes 3649536 | tf_op jit(solution)/shard_map/all_gather | solution.py:83
  9.0 122.1 %all-gather.7.cloned.1.call-start = ((), (), s32[]{:S(2)}) async-start(), calls=%async_computation.5 | async-start | bytes 1216512 | tf_op jit(solution)/shard_map/all_gather | solution.py:86
  10.5 186.5 %all-gather.9.cloned.1.call-start = ((), (), s32[]{:S(2)}) async-start(), calls=%async_computation.6 | async-start | bytes 4866048 | tf_op jit(solution)/shard_map/all_gather | solution.py:139
  12.3 250.1 %all-gather.11.cloned.1.call-start = ((), (), s32[]{:S(2)}) async-start(), calls=%async_computation.7 | async-start | bytes 4866048 | tf_op jit(solution)/shard_map/all_gather | solution.py:163
  14.0 668.9 %reduce-scatter.7.cloned.1.call-start = ((), (), s32[]{:S(2)}) async-start(), calls=%async_computation.9 | async-start | bytes 2433024 | tf_op jit(solution)/shard_map/reduce_scatter | solution.py:249
  65.0 15.2 %copy-start.31 = (f32[768]{0:T(1024)}, f32[768]{0:T(1024)S(1)}, u32[]{:S(2)}) copy-start(f32[768]{0:T(1024)S(1)} %convert_element_type.135) | copy-start | bytes 9220
  66.8 13.5 %copy-start.33 = (f32[864]{0:T(1024)}, f32[864]{0:T(1024)S(1)}, u32[]{:S(2)}) copy-start(f32[864]{0:T(1024)S(1)} %div.39) | copy-start | bytes 10372
  67.4 0.6 copy-start.39
  67.4 12.9 %copy-start.35 = (f32[864]{0:T(1024)}, f32[864]{0:T(1024)S(1)}, u32[]{:S(2)}) copy-start(f32[864]{0:T(1024)S(1)} %rsqrt.20) | copy-start | bytes 10372
  68.1 128.9 %copy-start.28 = (f32[768]{0:T(1024)}, f32[768]{0:T(1024)S(1)}, u32[]{:S(2)}) copy-start(f32[768]{0:T(1024)S(1)} %convert_element_type.155) | copy-start | bytes 9220
  70.2 10.1 %copy-start.22 = (bf16[864,768]{1,0:T(8,128)(2,1)}, bf16[864,768]{1,0:T(8,128)(2,1)S(1)}, u32[]{:S(2)}) copy-start(bf16[864,768]{1,0:T(8,128)(2,1)S(1)} %add_convert_fusion.5) | copy-start | bytes 3981316
  86.5 18.5 %copy-start.2 = (bf16[3,8,36,12,64]{4,3,2,1,0:T(8,128)(2,1)}, bf16[3,8,36,12,64]{4,3,2,1,0:T(8,128)(2,1)S(1)}, u32[]{:S(2)}) copy-start(bf16[3,8,36,12,64]{4,3,2,1,0:T(8,128)(2,1)S(1)} %reshape.190) | copy-start | bytes 3981316
  97.2 5.4 copy-start.18
  102.7 2.5 copy-start
  105.2 2.5 copy-start.16
  134.8 71.7 %copy-start.37 = (f32[864]{0:T(1024)}, f32[864]{0:T(1024)S(1)}, u32[]{:S(2)}) copy-start(f32[864]{0:T(1024)S(1)} %multiply_reduce_fusion.5) | copy-start | bytes 10372
  134.9 127.4 %copy-start.30 = (f32[3072]{0:T(1024)S(1)}, f32[3072]{0:T(1024)}, u32[]{:S(2)}) copy-start(f32[3072]{0:T(1024)} %convert_element_type.159) | copy-start | bytes 36868
  262.3 33.9 %copy-start.45 = (bf16[768,3072]{1,0:T(8,128)(2,1)S(1)}, bf16[768,3072]{1,0:T(8,128)(2,1)}, u32[]{:S(2)}) copy-start(bf16[768,3072]{1,0:T(8,128)(2,1)} %all-gather.9.cloned.1.call-done) | copy-start | bytes 14155780
  296.2 5.3 copy-start.12
  296.2 5.3 copy-start.38
  301.5 2.5 copy-start.6
  302.5 1.5 copy-start.3
  302.5 3.0 copy-start.24
  304.5 1.1 copy-start.25
  312.3 5.3 copy-start.17
  312.3 5.3 copy-start.19
  327.8 355.1 %reduce-scatter.5.cloned.1.call-start = ((), (), s32[]{:S(2)}) async-start(), calls=%async_computation.8 | async-start | bytes 7299072 | tf_op jit(solution)/shard_map/reduce_scatter | solution.py:246
  327.9 5.9 copy-start.9
  333.8 2.0 copy-start.1
  370.6 1.7 copy-start.15
  370.6 2.1 copy-start.8
  372.3 2.5 copy-start.23
  372.8 2.0 copy-start.26
  380.8 0.7 copy-start.29
  380.8 386.0 %reduce-scatter.9.cloned.1.call-start = ((), (), s32[]{:S(2)}) async-start(), calls=%async_computation.10 | async-start | bytes 9732096 | tf_op jit(solution)/shard_map/reduce_scatter | solution.py:183
  392.1 516.4 %reduce-scatter.11.cloned.1.call-start = ((), (), s32[]{:S(2)}) async-start(), calls=%async_computation.11 | async-start | bytes 9732096 | tf_op jit(solution)/shard_map/reduce_scatter | solution.py:185
  392.1 11.0 %copy-start.7 = (bf16[3,288,768]{2,1,0:T(8,128)(2,1)S(1)}, bf16[3,288,768]{2,1,0:T(8,128)(2,1)}, u32[]{:S(2)}) copy-start(bf16[3,288,768]{2,1,0:T(8,128)(2,1)} %param.18) | copy-start | bytes 3981316
  400.7 2.4 copy-start.14
  410.8 1.0 copy-start.21
  411.8 1.4 collective-permute-start
  413.3 9.4 %collective-permute-start.1 = (bf16[2,96,768]{2,1,0:T(8,128)(2,1)S(1)}, bf16[2,96,768]{2,1,0:T(8,128)(2,1)}, u32[]{:S(2)}, u32[]{:S(2)}) collective-permute-start(bf16[2,96,768]{2,1,0:T(8,128)(2,1)S(1)} %pad_maximum_fusion.4), channel_id=1, source_target_pairs={{0,2},{1,3},{2,0},{3,1},{4,6},{5,7},{6,4},{7,5},{8,10},{9,11},{10,... | collective-permute-start | bytes 884744 | tf_op jit(solution)/shard_map/ppermute | solution.py:23
  423.7 2.4 copy-start.20
  424.6 15.0 %collective-permute-start.2 = (bf16[4,96,768]{2,1,0:T(8,128)(2,1)}, bf16[4,96,768]{2,1,0:T(8,128)(2,1)}, u32[]{:S(2)}, u32[]{:S(2)}) collective-permute-start(bf16[4,96,768]{2,1,0:T(8,128)(2,1)} %pad_maximum_fusion.3), channel_id=1, source_target_pairs={{0,4},{1,5},{2,6},{3,7},{4,0},{5,1},{6,2},{7,3},{8,12},{9,13},{10,... | collective-permute-start | bytes 1769480 | tf_op jit(solution)/shard_map/ppermute | solution.py:23
  440.9 0.8 copy-start.13
  442.8 26.8 %collective-permute-start.3 = (bf16[8,96,768]{2,1,0:T(8,128)(2,1)}, bf16[8,96,768]{2,1,0:T(8,128)(2,1)}, u32[]{:S(2)}, u32[]{:S(2)}) collective-permute-start(bf16[8,96,768]{2,1,0:T(8,128)(2,1)} %pad_maximum_fusion.2), channel_id=1, source_target_pairs={{0,8},{1,9},{2,10},{3,11},{4,12},{5,13},{6,14},{7,15},{8,0},{9,1},... | collective-permute-start | bytes 3538952 | tf_op jit(solution)/shard_map/ppermute | solution.py:23
  471.2 1.0 copy-start.10
  471.2 2.7 copy-start.11
  471.2 4.5 copy-start.44
  473.9 131.1 %collective-permute-start.4 = (bf16[16,96,768]{2,1,0:T(8,128)(2,1)}, bf16[16,96,768]{2,1,0:T(8,128)(2,1)}, u32[]{:S(2)}, u32[]{:S(2)}) collective-permute-start(bf16[16,96,768]{2,1,0:T(8,128)(2,1)} %pad_maximum_fusion.1), channel_id=1, source_target_pairs={{0,16},{1,17},{2,18},{3,19},{4,20},{5,21},{6,22},{7,23},{8,24},{9,... | collective-permute-start | bytes 7077896 | tf_op jit(solution)/shard_map/ppermute | solution.py:23
  607.6 2.9 copy-start.5
  607.6 4.3 copy-start.27
  607.6 4.3 copy-start.32
  607.7 4.3 copy-start.34
  607.7 4.3 copy-start.36
  607.7 5.4 copy-start.46
  613.0 3.9 copy-start.40
  619.1 5.2 copy-start.41
  619.1 5.2 copy-start.43
Sparse Core Ops, SparseCore 0:
  11.5 63.2 all-gather.4
  78.3 52.7 all-gather.6
  134.5 62.4 all-gather.8
  200.4 61.9 all-gather.10
  327.9 97.9 reduce-scatter.6
  432.0 192.9 reduce-scatter.4
  631.5 135.2 reduce-scatter.8
  773.2 135.1 reduce-scatter.10
